TPU v7x, 512 devices: a whole 4x4x16 slice. The times are simulated.
512 devices in a mesh: blk: 16 (over y_lo, x, core), grp: 32 (over z, y_hi).
Axes of the slice: x: 4, y: 4 (y_hi: 2, y_lo: 2; y = y_hi * 2 + y_lo), z: 16, core: 2. Of those that a mesh axis runs over, the one named last changes fastest.
Arguments:
- amps: bfloat16 [4096, 8, 512], P(('blk', 'grp')), may hold values from -6 to 6
- domains: int32 [4096, 8], replicated, may hold values from 0 to 15, all different within a row
- owner: int32 [4096], replicated, may hold values from 0 to 4095, as said below
- coupling: int32 [16, 16], replicated, may hold values from 0 to 1, as said below
- integrals: bfloat16 [8192, 8192], P('blk', 'grp'), may hold values from -0.125 to 0.125
Outputs:
- residual: float32 [4096, 8192], P('blk', 'grp')
Inputs may be any that keep to these rules, and one draw needn't show every extreme that they name: `domains`: each row names 8 different pair blocks, and every block is named by some row. owner maps the occupied pairs of each group of 256 consecutive pairs one to one onto the slots of the same group. Every column of coupling holds exactly 8 ones.
All inputs are finite; a program needn't handle non-finite values.
Results may differ from a plain program's by a relative error of at most 0.0003.
Values may be sent and summed in bfloat16 or wider, within the bound.
No kernel may reach another device: no remote copies, remote signals or barrier semaphores. Data moves between devices by JAX's collectives and lax.ppermute only.
A program may use at most 64 MiB of HBM per device.

v0:
```python
import jax
import jax.numpy as jnp
from jax import lax
from jax.sharding import PartitionSpec as P


def on_device(amps, domains, owner, coupling, integrals):
    n_blk = lax.axis_size("blk")
    me_blk = lax.axis_index("blk")
    me_grp = lax.axis_index("grp")
    block_rows, col_count = integrals.shape
    col_split = block_rows // col_count
    nvb = coupling.shape[0]
    op_total = owner.shape[0]
    op_grp = op_total // n_blk
    dom_width = domains.shape[1]
    target = me_grp // col_split
    blocks = jnp.arange(nvb, dtype=jnp.int32)
    keep_col = lax.dynamic_index_in_dim(coupling, target, axis=1, keepdims=False)
    group_base = me_blk * op_grp
    own_pairs = lax.dynamic_slice_in_dim(owner, group_base, op_grp)
    local_slots = own_pairs - group_base
    group_dom = lax.dynamic_slice_in_dim(domains, group_base, op_grp)
    permuter = (local_slots[:, None] == jnp.arange(op_grp, dtype=jnp.int32)[None, :]).astype(
        jnp.float32
    )
    pair_dom = jnp.dot(
        permuter, group_dom.astype(jnp.float32), precision=lax.Precision.HIGHEST
    ).astype(jnp.int32)
    in_domain = jnp.any(pair_dom == target, axis=1).astype(jnp.float32)
    group_amps = lax.all_gather(amps, "grp", axis=0, tiled=True)
    flat_amps = group_amps.reshape(op_grp, dom_width * block_rows)
    ordered = jnp.take(flat_amps, local_slots, axis=0).reshape(op_grp, dom_width, block_rows)
    selector = (pair_dom[:, :, None] == blocks[None, None, :]) & (keep_col[None, None, :] > 0)
    tile_full = jnp.einsum(
        "pkc,pkx->pcx", selector.astype(jnp.bfloat16), ordered, preferred_element_type=jnp.float32
    )
    tile_full = tile_full.astype(jnp.bfloat16).reshape(op_grp, nvb * block_rows)
    summed = jnp.dot(
        tile_full,
        lax.all_gather(integrals, "blk", axis=0, tiled=True),
        preferred_element_type=jnp.float32,
    )
    return summed * in_domain[:, None]


def solution(mesh):
    return jax.shard_map(
        on_device,
        mesh=mesh,
        in_specs=(P(("blk", "grp"), None, None), P(), P(), P(), P("blk", "grp")),
        out_specs=P("blk", "grp"),
        check_vma=False,
    )
```

profile of v0, /device:TPU:1, one launch (start us, length us, event | category | flops | bytes accessed | tf_op | source)
XLA Modules:
  0.0 219.4 jit_solution(15730783104113241704)
XLA Ops:
  6.5 0.0 all-gather.3.cloned.1.call-start
  6.5 0.7 all-gather.3.cloned.1.call-update
  7.3 0.0 all-gather.5.cloned.1.call-start
  7.3 0.7 all-gather.5.cloned.1.call-update
  8.0 0.8 compare_and_fusion
  8.8 1.0 compare_reduce_fusion
  9.8 0.1 copy.8
  10.0 0.9 fusion.7
  10.9 145.2 %all-gather.3.cloned.1.call-done = bf16[256,8,512]{2,1,0:T(8,128)(2,1)} async-done(((bf16[8,8,512]{2,1,0:T(8,128)(2,1)}), bf16[256,8,512]{2,1,0:T(8,128)(2,1)}) %all-gather.3.cloned.1.call-update) | async-done | bytes 2097168 | tf_op jit(solution)/shard_map/all_gather | solution.py:31
  156.1 2.5 %copy.9 = bf16[32,8,8,512]{3,1,2,0:T(8,128)(2,1)S(1)} copy(bf16[32,8,8,512]{3,2,1,0:T(8,128)(2,1)} %bitcast.14) | data formatting | bytes 4194304
  158.6 3.2 %gather_fusion = bf16[256,4096]{1,0:T(8,128)(2,1)} fusion(bf16[256,4096]{1,0:T(8,128)(2,1)S(1)} %bitcast.10, s32[1024]{0:T(1024)S(1)} %pad_clamp_fusion), kind=kCustom, calls=%fused_computation | custom fusion | bytes 4195328 | tf_op jit(solution)/shard_map/jit(_take)/gather | solution.py:33
  161.7 2.5 %copy.10 = bf16[32,8,8,512]{3,2,1,0:T(8,128)(2,1)S(1)} copy(bf16[32,8,8,512]{3,1,2,0:T(8,128)(2,1)} %bitcast.12) | data formatting | bytes 4194304
  164.2 1.1 bitcast_select_fusion
  165.3 3.7 %convolution_convert_fusion = bf16[256,16,512]{2,1,0:T(8,128)(2,1)S(1)} fusion(bf16[256,8,512]{2,1,0:T(8,128)(2,1)S(1)} %bitcast_select_fusion, s32[256,8]{1,0:T(8,128)S(1)} %copy.8, pred[16]{0:T(512)(128)(4,1)S(1)} %fusion.7), kind=kOutput, calls=%fused_computation.1 | convolution fusion | flops 35717120 | bytes 6299664 | tf_op jit(solution)/shard_map/pkc,pkx->pcx/dot_general | solution.py:35
  169.1 6.3 %copy.11 = bf16[32,8,16,512]{3,1,2,0:T(8,128)(2,1)} copy(bf16[32,8,16,512]{3,2,1,0:T(8,128)(2,1)S(1)} %bitcast.11) | data formatting | bytes 8388608
  175.3 31.8 %all-gather.5.cloned.1.call-done = bf16[8192,256]{1,0:T(8,128)(2,1)} async-done(((bf16[512,256]{1,0:T(8,128)(2,1)}), bf16[8192,256]{1,0:T(8,128)(2,1)}) %all-gather.5.cloned.1.call-update) | async-done | bytes 4194320 | tf_op jit(solution)/shard_map/all_gather | solution.py:41
  207.1 5.4 %convolution_multiply_fusion = f32[256,256]{1,0:T(8,128)} fusion(bf16[256,8192]{1,0:T(8,128)(2,1)} %bitcast.13, bf16[8192,256]{1,0:T(8,128)(2,1)} %all-gather.5.cloned.1.call-done, f32[256]{0:T(256)S(1)} %convert_element_type.21), kind=kOutput, calls=%fused_computation.3 | convolution fusion | flops 1073807360 | bytes 8651776 | tf_op jit(solution)/shard_map/dot_general | solution.py:39
  (3 shorter events, 0.0 us)
Async XLA Ops:
  6.5 149.5 %all-gather.3.cloned.1.call-start = ((), (), s32[]{:S(2)}) async-start(), calls=%async_computation | async-start | bytes 2162688 | tf_op jit(solution)/shard_map/all_gather | solution.py:31
  7.3 199.9 %all-gather.5.cloned.1.call-start = ((), (), s32[]{:S(2)}) async-start(), calls=%async_computation.1 | async-start | bytes 4456448 | tf_op jit(solution)/shard_map/all_gather | solution.py:41
Sparse Core Ops, SparseCore 0:
  10.4 145.5 all-gather.2
  158.2 48.8 all-gather.4
where the time goes:
time: 220 us; the launch traced here: 219 us
  waiting for transfers between devices  178 us (81%)
  local copies, waits for them, and re-layouts  14.5 us (7%)
  between operations  13.5 us (6%)
  matrix products  10.2 us (5%)
  other arithmetic  2.75 us (1%)
    all_gather x1, waiting for transfers between devices, on_device(): group_amps = lax.all_gather(amps, 'grp', axis=0, tiled=True)  145 us
    all_gather x1, waiting for transfers between devices, on_device(): lax.all_gather(integrals, 'blk', axis=0, tiled=True)  31.8 us
    unnamed x3, local copies, waits for them, and re-layouts  11.2 us
    dot_general x1, matrix products, on_device(): jnp.dot(tile_full, lax.all_gather(integrals, 'blk', axis=0, tiled=True),...  5.42 us
  transfers between devices with their start and end apart: 2, of which 2 were waited for; matrix products, arithmetic and copies ran while one was open for 10% of the time, Pallas kernels for 0%

commit v1 on v0

--- a/solution.py
+++ b/solution.py
@@ -38,7 +38,9 @@
     tile_full = tile_full.astype(jnp.bfloat16).reshape(op_grp, nvb * block_rows)
     summed = jnp.dot(
         tile_full,
-        lax.all_gather(integrals, "blk", axis=0, tiled=True),
+        jnp.concatenate(
+            lax.all_to_all(jnp.stack([integrals] * lax.axis_size("blk")), "blk", 0, 0), axis=0
+        ),
         preferred_element_type=jnp.float32,
     )
     return summed * in_domain[:, None]

time: 220 us -> 205 us (0.932)
  the two profiles are of different devices: /device:TPU:1 before, /device:TPU:2 now
where the time goes in v1:
time: 205 us
  waiting for transfers between devices  153 us (75%)
  matrix products  14.9 us (7%)
  between operations  13.4 us (7%)
  local copies, waits for them, and re-layouts  11.6 us (6%)
  starting transfers between devices  10.3 us (5%)
  other arithmetic  2.06 us (1%)
    all_gather x1, waiting for transfers between devices, on_device(): group_amps = lax.all_gather(amps, 'grp', axis=0, tiled=True)  152 us
    all_to_all x1, starting transfers between devices, on_device(): lax.all_to_all(jnp.stack([integrals] * lax.axis_size('blk')), 'blk', 0, 0)  10.3 us
    dot_general x1, matrix products, on_device(): jnp.dot(tile_full, jnp.concatenate(lax.all_to_all(jnp.stack([integrals] *...  8.87 us
    dot_general x1, matrix products, on_device(): jnp.einsum('pkc,pkx->pcx', selector.astype(jnp.bfloat16), ordered, prefer...  5.04 us
    unnamed x4, local copies, waits for them, and re-layouts  4.97 us
  transfers between devices with their start and end apart: 2, of which 1 were waited for; matrix products, arithmetic and copies ran while one was open for 10% of the time, Pallas kernels for 0%

profile of v1, /device:TPU:2, one launch (start us, length us, event | category | flops | bytes accessed | tf_op | source)
XLA Modules:
  0.0 205.0 jit_solution(12593773195904983348)
XLA Ops:
  6.5 0.0 all-gather.2.cloned.1.call-start
  6.5 0.7 all-gather.2.cloned.1.call-update
  7.3 3.3 %stack.2 = bf16[16,512,256]{2,1,0:T(8,128)(2,1)} broadcast(bf16[512,256]{1,0:T(8,128)(2,1)} %param.9), dimensions={1,2} | broadcast | bytes 4456448 | tf_op jit(solution)/shard_map/stack | solution.py:42
  10.6 0.0 copy-start
  10.6 10.3 %all-to-all-start = ((bf16[16,512,256]{2,1,0:T(8,128)(2,1)}), bf16[16,512,256]{2,1,0:T(8,128)(2,1)}, u32[]{:S(2)}, u32[]{:S(2)}) async-start(bf16[16,512,256]{2,1,0:T(8,128)(2,1)} %stack.2), calls=%async_computation | async-start | bytes 8388608 | tf_op jit(solution)/shard_map/all_to_all | solution.py:42
  20.9 0.8 compare_and_fusion
  21.6 1.0 compare_reduce_fusion
  22.7 0.1 copy.8
  22.8 0.0 copy-done
  22.8 0.2 fusion.15
  23.0 151.9 %all-gather.2.cloned.1.call-done = bf16[256,8,512]{2,1,0:T(8,128)(2,1)} async-done(((bf16[8,8,512]{2,1,0:T(8,128)(2,1)}), bf16[256,8,512]{2,1,0:T(8,128)(2,1)}) %all-gather.2.cloned.1.call-update) | async-done | bytes 2097168 | tf_op jit(solution)/shard_map/all_gather | solution.py:31
  174.9 2.5 %copy.10 = bf16[32,8,8,512]{3,1,2,0:T(8,128)(2,1)S(1)} copy(bf16[32,8,8,512]{3,2,1,0:T(8,128)(2,1)} %bitcast.13) | data formatting | bytes 4194304
  177.4 3.2 %gather_fusion = bf16[256,4096]{1,0:T(8,128)(2,1)} fusion(bf16[256,4096]{1,0:T(8,128)(2,1)S(1)} %bitcast.11, s32[1024]{0:T(1024)S(1)} %pad_clamp_fusion), kind=kCustom, calls=%fused_computation | custom fusion | bytes 4195328 | tf_op jit(solution)/shard_map/jit(_take)/gather | solution.py:33
  180.6 2.5 %copy.11 = bf16[32,8,8,512]{3,2,1,0:T(8,128)(2,1)S(1)} copy(bf16[32,8,8,512]{3,1,2,0:T(8,128)(2,1)} %bitcast.12) | data formatting | bytes 4194304
  183.1 1.1 bitcast_select_fusion
  184.2 5.0 %convolution_convert_fusion = bf16[256,16,512]{2,1,0:T(8,128)(2,1)} fusion(bf16[256,8,512]{2,1,0:T(8,128)(2,1)S(1)} %bitcast_select_fusion, s32[256,8]{1,0:T(8,128)S(1)} %copy.8, pred[16]{0:T(512)(128)(4,1)S(1)} %fusion.15), kind=kOutput, calls=%fused_computation.3 | convolution fusion | flops 35717120 | bytes 6299664 | tf_op jit(solution)/shard_map/pkc,pkx->pcx/dot_general | solution.py:35
  189.3 0.0 all-to-all-done
  189.3 8.9 %fusion.5 = f32[256,256]{1,0:T(8,128)} fusion(bf16[16,512,256]{2,1,0:T(8,128)(2,1)} %all-to-all-done, bf16[256,16,512]{2,1,0:T(8,128)(2,1)} %convolution_convert_fusion, f32[256]{0:T(256)S(1)} %convert_element_type.21), kind=kOutput, calls=%fused_computation.6 | convolution fusion | flops 1073807360 | bytes 8651776 | tf_op jit(solution)/shard_map/dot_general | solution.py:39
  (3 shorter events, 0.0 us)
Async XLA Ops:
  6.5 168.4 %all-gather.2.cloned.1.call-start = ((), (), s32[]{:S(2)}) async-start(), calls=%async_computation.1 | async-start | bytes 2162688 | tf_op jit(solution)/shard_map/all_gather | solution.py:31
  10.6 12.2 %copy-start = (s32[16,16]{1,0:T(8,128)S(1)}, s32[16,16]{1,0:T(8,128)}, u32[]{:S(2)}) copy-start(s32[16,16]{1,0:T(8,128)} %param.8) | copy-start | bytes 3076
  10.6 178.7 %all-to-all-start = ((bf16[16,512,256]{2,1,0:T(8,128)(2,1)}), bf16[16,512,256]{2,1,0:T(8,128)(2,1)}, u32[]{:S(2)}, u32[]{:S(2)}) async-start(bf16[16,512,256]{2,1,0:T(8,128)(2,1)} %stack.2), calls=%async_computation | async-start | bytes 8388608 | tf_op jit(solution)/shard_map/all_to_all | solution.py:42
Sparse Core Ops, SparseCore 0:
  10.4 164.4 all-gather.1
